TPU v7x, 128 devices: a whole 4x4x4 slice. The times are simulated.
128 devices in a mesh: req: 4 (over y), exp: 32 (over z, x, core).
Axes of the slice: x: 4, y: 4, z: 4, core: 2. Of those that a mesh axis runs over, the one named last changes fastest.
Arguments:
- hidden: bfloat16 [8, 2048, 2048], P('req', 'exp'), may hold values from -6 to 6
- q_new: bfloat16 [8, 16, 2048, 128], P('req', None, 'exp'), may hold values from -480 to 480
- k_new: bfloat16 [8, 16, 2048, 128], P('req', None, 'exp'), may hold values from -6 to 6
- v_new: bfloat16 [8, 16, 2048, 128], P('req', None, 'exp'), may hold values from -6 to 6
- routes: int32 [8, 2048, 6], P('req', 'exp'), may hold values from 0 to 63, all different within a row; in each aligned block of 64 rows (0 to 63, 64 to 127, ..., all dimensions but the last counted through in order) at most 8 rows name the same one
- slot_request: int32 [8], replicated, may hold values from 0 to 7, each once
- lengths: int32 [8], replicated, may hold values from 5 to 16384, as said below
- cycle_cache: bfloat16 [128, 2, 4096, 128], P(('req', 'exp')), may hold values from -6 to 6
- sink_cache: bfloat16 [128, 2, 4, 128], P(('req', 'exp')), may hold values from -6 to 6
- w_out: bfloat16 [2048, 2048], replicated, may hold values from -0.125 to 0.125
- norm_gain: float32 [2048], replicated, may hold values from 0.5 to 1.5
- router: bfloat16 [2048, 64], replicated, may hold values from -0.125 to 0.125
- w_gate: bfloat16 [2048, 90112], P(None, ('req', 'exp')), may hold values from -0.125 to 0.125
- w_up: bfloat16 [2048, 90112], P(None, ('req', 'exp')), may hold values from -0.125 to 0.125
- w_down: bfloat16 [90112, 2048], P(('req', 'exp')), may hold values from -0.15625 to 0.15625
Outputs:
- layer_out: bfloat16 [8, 2048, 2048], P('req', 'exp')
- cycle_out: bfloat16 [128, 2, 4096, 128], P(('req', 'exp'))
Inputs may be any that keep to these rules, and one draw needn't show every extreme that they name: In every aligned block of 64 rows of routes (the rows of one request on one index of exp) no expert is named by more than 8 rows, a bound that some block reaches. `slot_request`: each request once. `lengths`: some slot has exactly 16384 cached tokens, and some other fewer than 2048.
All inputs are finite; a program needn't handle non-finite values.
Results may differ from a plain program's by a relative error of at most 0.014.
The roundings to bfloat16 on the way count: a program that leaves them out, or rounds other values in their place, can miss the bound.
Values may be sent and summed in bfloat16 or wider, within the bound.
No kernel may reach another device: no remote copies, remote signals or barrier semaphores. Data moves between devices by JAX's collectives and lax.ppermute only.
A program may use at most 192 MiB of HBM per device.

v0:
```python
import jax
import jax.numpy as jnp
from jax import lax
from jax.sharding import PartitionSpec as P

SPLIT = 2


def for_sending(array):

    def short(part):
        return part.astype(jnp.bfloat16) if part.dtype == jnp.float32 else part

    return jax.tree.map(short, array)


def rotate(vectors, positions):
    half_width = vectors.shape[-1] // 2
    frequency = 10000.0 ** (-2.0 * jnp.arange(half_width, dtype=jnp.float32) / vectors.shape[-1])
    angles = positions.astype(jnp.float32)[:, None] * frequency[None, :]
    cosine = jnp.cos(angles)
    sine_part = jnp.sin(angles)
    low_half = vectors[..., :half_width]
    high_half = vectors[..., half_width:]
    return jnp.concatenate(
        [low_half * cosine - high_half * sine_part, high_half * cosine + low_half * sine_part],
        axis=-1,
    )


def attend_block(
    q_block, row_start, cycle_from, new_upto, ordered, k_rot, value_new, sink_pair, length
):
    window = ordered.shape[1]
    score_scale = q_block.shape[1] ** (-0.5)
    key_rows = jnp.concatenate([ordered[0, cycle_from:], k_rot], 0)
    value_rows = jnp.concatenate([ordered[1, cycle_from:], value_new], 0)
    row_ids = row_start + jnp.arange(q_block.shape[0], dtype=jnp.int32)
    cycle_cols = cycle_from + jnp.arange(window - cycle_from, dtype=jnp.int32)
    cycle_visible = (cycle_cols[None, :] > row_ids[:, None]) & (
        cycle_cols[None, :] >= window - length
    )
    new_visible = jnp.arange(new_upto, dtype=jnp.int32)[None, :] <= row_ids[:, None]
    visible = jnp.concatenate([cycle_visible, new_visible], 1)
    scores = (
        jnp.einsum("qd,kd->qk", q_block, key_rows, preferred_element_type=jnp.float32) * score_scale
    )
    scores = jnp.where(visible, scores, -jnp.inf)
    sink_scores = (
        jnp.einsum("qd,kd->qk", q_block, sink_pair[0], preferred_element_type=jnp.float32)
        * score_scale
    )
    sink_visible = (
        jnp.arange(sink_pair.shape[1], dtype=jnp.int32)[None, :]
        <= (length + row_ids - window)[:, None]
    )
    sink_scores = jnp.where(sink_visible, sink_scores, -jnp.inf)
    highest = jnp.maximum(jnp.max(scores, axis=1), jnp.max(sink_scores, axis=1))[:, None]
    weights = jnp.exp(scores - highest)
    sink_weights = jnp.exp(sink_scores - highest)
    denominator = jnp.sum(weights, axis=1) + jnp.sum(sink_weights, axis=1)
    blended = jnp.dot(weights.astype(jnp.bfloat16), value_rows, preferred_element_type=jnp.float32)
    blended = blended + jnp.dot(
        sink_weights.astype(jnp.bfloat16), sink_pair[1], preferred_element_type=jnp.float32
    )
    return (blended / denominator[:, None]).astype(jnp.bfloat16)


def attend_pair(query_rows, key_new, value_new, cycle_pair, sink_pair, length):
    seq_len = query_rows.shape[0]
    window = cycle_pair.shape[1]
    block_rows = min(512, seq_len)
    positions = length + jnp.arange(seq_len, dtype=jnp.int32)
    q_rot = rotate(query_rows.astype(jnp.float32), positions).astype(jnp.bfloat16)
    k_rot = rotate(key_new.astype(jnp.float32), positions).astype(jnp.bfloat16)
    ordered = jnp.roll(cycle_pair, -(length % window), axis=1)
    outputs = []
    for block_number in range(seq_len // block_rows):
        row_start = block_number * block_rows
        cycle_from = 0
        outputs.append(
            attend_block(
                q_rot[row_start : row_start + block_rows],
                row_start,
                cycle_from,
                seq_len,
                ordered,
                k_rot,
                value_new,
                sink_pair,
                length,
            )
        )
    context = jnp.concatenate(outputs, 0)
    retained = ordered[:, seq_len:]
    appended = jnp.stack([k_rot, value_new])
    updated = jnp.roll(
        jnp.concatenate([retained, appended], 1), (length + seq_len) % window, axis=1
    )
    return (context, updated)


def on_device(
    hidden,
    q_new,
    k_new,
    v_new,
    routes,
    slot_request,
    lengths,
    cycle_cache,
    sink_cache,
    w_out,
    norm_gain,
    router,
    w_gate,
    w_up,
    w_down,
):
    group_width = lax.axis_size("exp")
    group_count = lax.axis_size("req")
    devices_all = group_count * group_width
    group_index = lax.axis_index("req")
    member_index = lax.axis_index("exp")
    slots_here, local_rows, model_width = hidden.shape
    head_count = q_new.shape[1]
    head_dim = q_new.shape[3]
    experts_all = router.shape[1]
    arrived = (
        lax.all_gather(hidden, "req", axis=0, tiled=True),
        lax.all_gather(q_new, "req", axis=0, tiled=True),
        lax.all_gather(k_new, "req", axis=0, tiled=True),
        lax.all_gather(v_new, "req", axis=0, tiled=True),
        lax.all_gather(routes, "req", axis=0, tiled=True),
    )
    requests = lax.dynamic_slice_in_dim(slot_request, group_index * slots_here, slots_here)
    hidden_sel, query_sel, key_sel, value_sel, route_sel = [
        jnp.take(arrival, requests, axis=0) for arrival in arrived
    ]
    pair_count = slots_here * head_count
    query_pairs, key_pairs, value_pairs = (
        lax.all_to_all(
            query_sel.reshape(pair_count, local_rows, head_dim),
            "exp",
            split_axis=0,
            concat_axis=1,
            tiled=True,
        ),
        lax.all_to_all(
            key_sel.reshape(pair_count, local_rows, head_dim),
            "exp",
            split_axis=0,
            concat_axis=1,
            tiled=True,
        ),
        lax.all_to_all(
            value_sel.reshape(pair_count, local_rows, head_dim),
            "exp",
            split_axis=0,
            concat_axis=1,
            tiled=True,
        ),
    )
    pairs_here = pair_count // group_width
    pair_ids = member_index * pairs_here + jnp.arange(pairs_here, dtype=jnp.int32)
    pair_lengths = jnp.take(lengths, group_index * slots_here + pair_ids // head_count)
    context, cycle_out = lax.map(
        lambda packed: attend_pair(*packed),
        (query_pairs, key_pairs, value_pairs, cycle_cache, sink_cache, pair_lengths),
    )
    context_rows = jax.tree.map(
        lambda part, own: part.astype(own.dtype),
        lax.all_to_all(for_sending(context), "exp", split_axis=1, concat_axis=0, tiled=True),
        context,
    ).reshape(slots_here, head_count, local_rows, head_dim)
    projected = jnp.einsum(
        "shqd,hde->sqe",
        context_rows,
        w_out.reshape(head_count, head_dim, model_width),
        preferred_element_type=jnp.float32,
    )
    residual = hidden_sel.astype(jnp.float32) + projected
    inverse = lax.rsqrt(jnp.mean(residual * residual, axis=-1, keepdims=True) + 1e-06)
    normed = (residual * inverse * norm_gain).astype(jnp.bfloat16)
    logits = jnp.einsum("sqd,de->sqe", normed, router, preferred_element_type=jnp.float32)
    gates = jax.nn.softmax(jnp.take_along_axis(logits, route_sel, axis=2), axis=-1)
    most_slots = max(2, local_rows // 8)
    expert_ids = jnp.arange(experts_all, dtype=jnp.int32)
    per_row = jnp.any(route_sel[..., None] == expert_ids, axis=2).astype(jnp.int32)
    earlier = jnp.cumsum(per_row, axis=1) - per_row
    ranks = jnp.take_along_axis(earlier, route_sel, axis=2)
    slot_ids = jnp.broadcast_to(
        jnp.arange(slots_here, dtype=jnp.int32)[:, None, None], route_sel.shape
    )
    spread = jnp.broadcast_to(normed[:, :, None, :], route_sel.shape + (model_width,))
    buffer = (
        jnp.zeros((experts_all, slots_here, most_slots, model_width), jnp.bfloat16)
        .at[route_sel, slot_ids, ranks]
        .set(spread)
    )
    sub_here = experts_all * SPLIT // devices_all
    piece_shape = (devices_all, sub_here, slots_here, most_slots, model_width)
    half_units = w_gate.shape[1] // sub_here
    gate_local = w_gate.reshape(model_width, sub_here, half_units)
    up_local = w_up.reshape(model_width, sub_here, half_units)
    down_local = w_down.reshape(sub_here, half_units, model_width)
    outgoing = jnp.broadcast_to(
        buffer[:, None], (experts_all, SPLIT, slots_here, most_slots, model_width)
    ).reshape(piece_shape)
    received = lax.all_to_all(outgoing, ("req", "exp"), split_axis=0, concat_axis=0, tiled=True)
    gate_part = jnp.einsum(
        "nsrkd,dsf->nsrkf", received, gate_local, preferred_element_type=jnp.float32
    )
    up_part = jnp.einsum("nsrkd,dsf->nsrkf", received, up_local, preferred_element_type=jnp.float32)
    active = (jax.nn.silu(gate_part) * up_part).astype(jnp.bfloat16)
    returned = lax.all_to_all(
        jnp.einsum(
            "nsrkf,sfd->nsrkd", active, down_local, preferred_element_type=jnp.float32
        ).astype(jnp.bfloat16),
        ("req", "exp"),
        split_axis=0,
        concat_axis=0,
        tiled=True,
    )
    pieces = returned.reshape(experts_all, SPLIT, slots_here, most_slots, model_width).astype(
        jnp.float32
    )
    summed = jnp.sum(pieces, axis=1)
    picked = summed[route_sel, slot_ids, ranks]
    moe = jnp.sum(gates[..., None] * picked, axis=2)
    layer_out = (residual + moe).astype(jnp.bfloat16)
    return (layer_out, cycle_out)


def solution(mesh):
    in_specs = (
        P("req", "exp", None),
        P("req", None, "exp", None),
        P("req", None, "exp", None),
        P("req", None, "exp", None),
        P("req", "exp", None),
        P(),
        P(),
        P(("req", "exp"), None, None, None),
        P(("req", "exp"), None, None, None),
        P(),
        P(),
        P(),
        P(None, ("req", "exp")),
        P(None, ("req", "exp")),
        P(("req", "exp"), None),
    )
    out_specs = (P("req", "exp", None), P(("req", "exp"), None, None, None))
    return jax.shard_map(
        on_device, mesh=mesh, in_specs=in_specs, out_specs=out_specs, check_vma=False
    )
```

profile of v0, /device:TPU:10, one launch (start us, length us, event | category | flops | bytes accessed | tf_op | source)
XLA Modules:
  0.0 760.1 jit_solution(11624940726540011022)
XLA Ops:
  14.7 12.3 %all_gather.19 = s32[8,64,6]{1,2,0:T(8,128)S(1)} all-gather(s32[2,64,6]{1,2,0:T(8,128)S(1)} %copy.55), channel_id=1, replica_groups=mesh['req'=4,'exp'=32] {'req'}, dimensions={0}, use_global_device_ids=true | all-gather | bytes 15360 | tf_op jit(solution)/shard_map/all_gather | solution.py:134
  37.6 8.3 %fusion.13 = (pred[512,4096]{1,0:T(32,128)(4,1)}, pred[512,4096]{1,0:T(32,128)(4,1)}, pred[512,4096]{1,0:T(32,128)(4,1)}, pred[512,4096]{1,0:T(32,128)(4,1)}) fusion(pred[4096]{0:T(1024)(128)(4,1)S(1)} %iota_compare_fusion.9, s32[512]{0:T(512)S(1)} %iota_add_fusion.2, s32[512]{0:T(512)S(1)} %get-tuple-element.90, s32[512]{0:T(512)S(1)} %get-tuple-element.89), kind=kLoop, calls=%fused_computation.37 | loop fusion | flops 16777216 | bytes 8398848 | tf_op jit(solution)/shard_map/while/body/eval_jaxpr/and | solution.py:40
  48.2 26.1 %all-gather.9.cloned.1.call-done = bf16[8,16,64,128]{3,2,1,0:T(8,128)(2,1)} async-done(((bf16[2,16,64,128]{3,2,1,0:T(8,128)(2,1)}), bf16[8,16,64,128]{3,2,1,0:T(8,128)(2,1)}) %all-gather.9.cloned.1.call-update) | async-done | bytes 2097168 | tf_op jit(solution)/shard_map/all_gather | solution.py:132
  77.3 29.5 %all-gather.7.cloned.1.call-done = bf16[8,16,64,128]{3,2,1,0:T(8,128)(2,1)} async-done(((bf16[2,16,64,128]{3,2,1,0:T(8,128)(2,1)}), bf16[8,16,64,128]{3,2,1,0:T(8,128)(2,1)}) %all-gather.7.cloned.1.call-update) | async-done | bytes 2097168 | tf_op jit(solution)/shard_map/all_gather | solution.py:131
  112.3 7.6 all-to-all-start.1
  121.5 8.7 %all-to-all-done.1 = bf16[32,64,128]{2,1,0:T(8,128)(2,1)S(1)} async-done(((bf16[32,64,128]{2,1,0:T(8,128)(2,1)}), bf16[32,64,128]{2,1,0:T(8,128)(2,1)S(1)}, u32[]{:S(2)}, u32[]{:S(2)}) %all-to-all-start.1) | async-done | bytes 524320 | tf_op jit(solution)/shard_map/all_to_all | solution.py:149
  137.0 9.4 %all-to-all-done = bf16[32,64,128]{2,1,0:T(8,128)(2,1)} async-done(((bf16[32,64,128]{2,1,0:T(8,128)(2,1)}), bf16[32,64,128]{2,1,0:T(8,128)(2,1)}, u32[]{:S(2)}, u32[]{:S(2)}) %all-to-all-start) | async-done | bytes 524320 | tf_op jit(solution)/shard_map/all_to_all | solution.py:142
  152.6 7.5 fusion.78
  171.0 7.5 fusion.19
  186.9 8.4 %fusion.143 = (f32[512]{0:T(512)S(1)}, f32[512,6144]{1,0:T(8,128)S(1)}) fusion(bf16[512,128]{1,0:T(8,128)(2,1)S(1)} %copy-done.21, bf16[2048,64]{1,0:T(8,128)(2,1)} %copy-done.12, bf16[2048,64]{1,0:T(8,128)(2,1)S(1)} %copy-done.11, bf16[4096,128]{1,0:T(8,128)(2,1)} %get-tuple-element.45, pred[512,2048]{1,0:T(32,128)(4,1)} %iota_compare_fusion.6, ...), kind=kOutput, calls=%fused_computation.234 | convolution fusion | flops 822607360 | bytes 17434624 | tf_op jit(solution)/shard_map/while/body/eval_jaxpr/qd,kd->qk/dot_general | solution.py:46
  197.4 8.6 %fusion.145 = (f32[512]{0:T(512)S(1)}, f32[512,6144]{1,0:T(8,128)}) fusion(bf16[512,128]{1,0:T(8,128)(2,1)S(1)} %copy-done.20, bf16[2048,64]{1,0:T(8,128)(2,1)} %copy-done.12, bf16[2048,64]{1,0:T(8,128)(2,1)S(1)} %copy-done.11, bf16[4096,128]{1,0:T(8,128)(2,1)} %get-tuple-element.45, pred[512,2048]{1,0:T(32,128)(4,1)} %iota_compare_fusion.7, ...), kind=kOutput, calls=%fused_computation.236 | convolution fusion | flops 822607360 | bytes 17434624 | tf_op jit(solution)/shard_map/while/body/eval_jaxpr/qd,kd->qk/dot_general | solution.py:46
  220.0 8.9 %copy.87 = bf16[1,2048,128]{2,0,1:T(2,128)(2,1)} copy(bf16[1,2048,128]{2,1,0:T(8,128)(2,1)S(1)} %maximum_bitcast_fusion) | data formatting | bytes 1048576 | tf_op jit(solution)/shard_map/while/body/jit(dynamic_update_index_in_dim)/broadcast_in_dim | solution.py:167
  229.4 13.7 %reduce = bf16[2048,128]{1,0:T(8,128)(2,1)} reduce(bf16[2048,1,128]{2,1,0:T(2,128)(2,1)} %bitcast.188, bf16[]{:T(256)} %broadcast.485), dimensions={1}, to_apply=%bitcast.178.reduce_sub_computation | reduce | bytes 1048578
  245.1 7.6 all-to-all-start.3
  289.7 143.5 %scatter_fusion = bf16[64,2,8,2048]{3,2,1,0:T(8,128)(2,1)} fusion(bf16[64,2,8,2048]{3,2,1,0:T(8,128)(2,1)} %broadcast_in_dim.180, s32[768]{0:T(1024)S(1)} %reshape.373, bf16[768,2048]{1,0:T(8,128)(2,1)} %reshape.375), kind=kCustom, calls=%fused_computation.8 | custom fusion | bytes 9446400 | tf_op jit(solution)/shard_map/scatter | solution.py:199
  440.0 106.9 %all_to_all.49 = bf16[128,1,2,8,2048]{4,3,2,1,0:T(8,128)(2,1)S(1)} all-to-all(bf16[128,1,2,8,2048]{4,3,2,1,0:T(8,128)(2,1)} %bitcast.180), channel_id=1, replica_groups=mesh['req'=4,'exp'=32] {'req','exp'}, dimensions={0} | all-to-all | bytes 16777216 | tf_op jit(solution)/shard_map/all_to_all | solution.py:210
  550.2 12.8 %fusion.9 = f32[128,2,8,704]{0,3,2,1:T(8,128)} fusion(bf16[128,1,2,8,2048]{4,3,2,1,0:T(8,128)(2,1)S(1)} %all_to_all.49, bf16[2048,704]{0,1:T(8,128)(2,1)S(1)} %copy-done.34), kind=kOutput, calls=%fused_computation.27 | convolution fusion | flops 5905580032 | bytes 17039360 | tf_op jit(solution)/shard_map/nsrkd,dsf->nsrkf/dot_general | solution.py:214
  563.0 27.3 %convert_bitcast_fusion = bf16[128,1,2,8,2048]{4,0,3,2,1:T(8,128)(2,1)} fusion(bf16[704,2048]{1,0:T(8,128)(2,1)S(1)} %copy-done, f32[128,2,8,704]{0,3,2,1:T(8,128)} %fusion.9, bf16[128,1,2,8,2048]{4,3,2,1,0:T(8,128)(2,1)} %copy-done.7, bf16[2048,704]{0,1:T(8,128)(2,1)} %param.31), kind=kOutput, calls=%fused_computation.32 | convolution fusion | flops 11824005120 | bytes 28311552 | tf_op jit(solution)/shard_map/nsrkf,sfd->nsrkd/dot_general | solution.py:217
  590.3 11.2 %copy.62 = bf16[128,1,2,8,2048]{4,3,2,1,0:T(8,128)(2,1)} copy(bf16[128,1,2,8,2048]{4,0,3,2,1:T(8,128)(2,1)} %convert_bitcast_fusion) | data formatting | bytes 16777216 | tf_op jit(solution)/shard_map/convert_element_type | solution.py:219
  610.4 8.7 %fusion.44 = bf16[1,2,4096,128]{3,2,1,0:T(8,128)(2,1)} fusion(s32[]{:T(128)S(6)} %select_n.213, bf16[2,2048,128]{2,1,0:T(8,128)(2,1)} %slice.118, bf16[1,2048,64]{2,1,0:T(8,128)(2,1)} %bitcast.190, bf16[1,2048,64]{2,1,0:T(8,128)(2,1)} %bitcast.191, bf16[1,2048,128]{2,1,0:T(8,128)(2,1)S(1)} %bitcast.185), kind=kLoop, calls=%fused_computation.80 | loop fusion | flops 16777216 | bytes 4194308 | tf_op jit(solution)/shard_map/while/body/jit(dynamic_update_index_in_dim)/broadcast_in_dim | solution.py:167
  626.4 85.9 %all-to-all-done.5 = bf16[128,1,2,8,2048]{4,3,2,1,0:T(8,128)(2,1)} async-done(((bf16[128,1,2,8,2048]{4,3,2,1,0:T(8,128)(2,1)}), bf16[128,1,2,8,2048]{4,3,2,1,0:T(8,128)(2,1)}, u32[]{:S(2)}, u32[]{:S(2)}) %all-to-all-start.5) | async-done | bytes 8388640 | tf_op jit(solution)/shard_map/all_to_all | solution.py:216
  712.4 9.6 %convert_reduce_fusion = f32[64,2,8,2048]{3,2,1,0:T(8,128)} fusion(bf16[64,2,2,8,2048]{4,3,2,1,0:T(8,128)(2,1)} %bitcast.179), kind=kLoop, calls=%fused_computation.10 | loop fusion | flops 6291456 | bytes 16777216 | tf_op jit(solution)/shard_map/reduce_sum | solution.py:228
  722.0 15.5 %gather_fusion.2 = f32[768,2048]{1,0:T(8,128)} fusion(f32[64,2,8,2048]{3,2,1,0:T(8,128)} %convert_reduce_fusion, s32[768]{0:T(1024)S(1)} %reshape.355), kind=kCustom, calls=%fused_computation.5 | custom fusion | bytes 12592128 | tf_op jit(solution)/shard_map/gather | solution.py:229
  737.5 8.1 %reshape.358 = f32[2,64,6,2048]{3,2,1,0:T(8,128)} reshape(f32[768,2048]{1,0:T(8,128)} %gather_fusion.2) | data formatting | bytes 12582912 | tf_op jit(solution)/shard_map/gather | solution.py:229
  (178 shorter events, 150.6 us)
Async XLA Ops:
  7.2 555.8 %copy-start = (bf16[704,2048]{1,0:T(8,128)(2,1)S(1)}, bf16[704,2048]{1,0:T(8,128)(2,1)}, u32[]{:S(2)}) copy-start(bf16[704,2048]{1,0:T(8,128)(2,1)} %param.33) | copy-start | bytes 8650756
  7.2 38.8 %all-gather.11.cloned.1.call-start = ((), (), s32[]{:S(2)}) async-start(), calls=%async_computation.9 | async-start | bytes 2621440 | tf_op jit(solution)/shard_map/all_gather | solution.py:133
  7.9 66.4 %all-gather.9.cloned.1.call-start = ((), (), s32[]{:S(2)}) async-start(), calls=%async_computation.8 | async-start | bytes 2621440 | tf_op jit(solution)/shard_map/all_gather | solution.py:132
  8.7 98.1 %all-gather.7.cloned.1.call-start = ((), (), s32[]{:S(2)}) async-start(), calls=%async_computation.7 | async-start | bytes 2621440 | tf_op jit(solution)/shard_map/all_gather | solution.py:131
  9.4 253.0 %all-gather.5.cloned.1.call-start = ((), (), s32[]{:S(2)}) async-start(), calls=%async_computation.6 | async-start | bytes 2621440 | tf_op jit(solution)/shard_map/all_gather | solution.py:130
  14.0 95.8 %copy-start.29 = (pred[2]{0:T(512)(128)(4,1)}, pred[2]{0:T(512)(128)(4,1)S(1)}, u32[]{:S(2)}) copy-start(pred[2]{0:T(512)(128)(4,1)S(1)} %get-tuple-element.42) | copy-start | bytes 10
  14.0 92.8 %copy-start.31 = (s32[1024]{0:T(1024)}, s32[1024]{0:T(1024)S(1)}, u32[]{:S(2)}) copy-start(s32[1024]{0:T(1024)S(1)} %pad_clamp_fusion) | copy-start | bytes 12292
  27.6 225.1 %copy-start.27 = (s32[2,64,6]{1,2,0:T(8,128)}, s32[2,64,6]{1,2,0:T(8,128)S(1)}, u32[]{:S(2)}) copy-start(s32[2,64,6]{1,2,0:T(8,128)S(1)} %broadcast_select_fusion.3) | copy-start | bytes 9220
  112.3 17.9 %all-to-all-start.1 = ((bf16[32,64,128]{2,1,0:T(8,128)(2,1)}), bf16[32,64,128]{2,1,0:T(8,128)(2,1)S(1)}, u32[]{:S(2)}, u32[]{:S(2)}) async-start(bf16[32,64,128]{2,1,0:T(8,128)(2,1)} %bitcast.195), calls=%async_computation.1 | async-start | bytes 1048576 | tf_op jit(solution)/shard_map/all_to_all | solution.py:149
  130.2 16.2 %all-to-all-start = ((bf16[32,64,128]{2,1,0:T(8,128)(2,1)}), bf16[32,64,128]{2,1,0:T(8,128)(2,1)}, u32[]{:S(2)}, u32[]{:S(2)}) async-start(bf16[32,64,128]{2,1,0:T(8,128)(2,1)} %bitcast.194), calls=%async_computation | async-start | bytes 1048576 | tf_op jit(solution)/shard_map/all_to_all | solution.py:142
  146.4 24.5 %all-to-all-start.2 = ((bf16[32,64,128]{2,1,0:T(8,128)(2,1)}), bf16[32,64,128]{2,1,0:T(8,128)(2,1)S(1)}, u32[]{:S(2)}, u32[]{:S(2)}) async-start(bf16[32,64,128]{2,1,0:T(8,128)(2,1)} %bitcast.193), calls=%async_computation.2 | async-start | bytes 1048576 | tf_op jit(solution)/shard_map/all_to_all | solution.py:156
  152.5 8.7 %copy-start.33 = (bf16[1,2,4,128]{3,2,1,0:T(4,128)(2,1)S(1)}, bf16[1,2,4,128]{3,2,1,0:T(4,128)(2,1)}, u32[]{:S(2)}) copy-start(bf16[1,2,4,128]{3,2,1,0:T(4,128)(2,1)} %param.27) | copy-start | bytes 6148
  152.5 8.9 %copy-start.15 = (pred[512,4096]{1,0:T(32,128)(4,1)S(1)}, pred[512,4096]{1,0:T(32,128)(4,1)}, u32[]{:S(2)}) copy-start(pred[512,4096]{1,0:T(32,128)(4,1)} %get-tuple-element.61) | copy-start | bytes 6291460
  152.6 8.9 %copy-start.17 = (pred[512,2048]{1,0:T(32,128)(4,1)S(1)}, pred[512,2048]{1,0:T(32,128)(4,1)}, u32[]{:S(2)}) copy-start(pred[512,2048]{1,0:T(32,128)(4,1)} %iota_compare_fusion.4) | copy-start | bytes 3145732
  152.6 8.9 %copy-start.18 = (bf16[4096,128]{1,0:T(8,128)(2,1)S(1)}, bf16[4096,128]{1,0:T(8,128)(2,1)}, u32[]{:S(2)}) copy-start(bf16[4096,128]{1,0:T(8,128)(2,1)} %get-tuple-element.45) | copy-start | bytes 3145732
  170.9 7.7 %copy-start.11 = (bf16[2048,64]{1,0:T(8,128)(2,1)S(1)}, bf16[2048,64]{1,0:T(8,128)(2,1)}, u32[]{:S(2)}) copy-start(bf16[2048,64]{1,0:T(8,128)(2,1)} %copy-done.10) | copy-start | bytes 786436
  171.0 7.7 %copy-start.13 = (bf16[2048,64]{1,0:T(8,128)(2,1)S(1)}, bf16[2048,64]{1,0:T(8,128)(2,1)}, u32[]{:S(2)}) copy-start(bf16[2048,64]{1,0:T(8,128)(2,1)} %copy-done.12) | copy-start | bytes 786436
  171.0 7.7 %copy-start.14 = (pred[512,4096]{1,0:T(32,128)(4,1)S(1)}, pred[512,4096]{1,0:T(32,128)(4,1)}, u32[]{:S(2)}) copy-start(pred[512,4096]{1,0:T(32,128)(4,1)} %get-tuple-element.60) | copy-start | bytes 6291460
  171.0 7.7 %copy-start.16 = (pred[512,2048]{1,0:T(32,128)(4,1)S(1)}, pred[512,2048]{1,0:T(32,128)(4,1)}, u32[]{:S(2)}) copy-start(pred[512,2048]{1,0:T(32,128)(4,1)} %iota_compare_fusion.5) | copy-start | bytes 3145732
  245.1 20.4 %all-to-all-start.3 = ((bf16[32,2,4096]{2,1,0:T(2,128)(2,1)}), bf16[32,2,4096]{2,1,0:T(2,128)(2,1)}, u32[]{:S(2)}, u32[]{:S(2)}) async-start(bf16[32,2,4096]{2,1,0:T(2,128)(2,1)} %reshape.397), calls=%async_computation.3 | async-start | bytes 1048576 | tf_op jit(solution)/shard_map/all_to_all | solution.py:173
  440.0 110.2 %copy-start.34 = (bf16[2048,704]{0,1:T(8,128)(2,1)S(1)}, bf16[2048,704]{0,1:T(8,128)(2,1)}, u32[]{:S(2)}) copy-start(bf16[2048,704]{0,1:T(8,128)(2,1)} %param.32) | copy-start | bytes 8650756
  601.6 110.8 %all-to-all-start.5 = ((bf16[128,1,2,8,2048]{4,3,2,1,0:T(8,128)(2,1)}), bf16[128,1,2,8,2048]{4,3,2,1,0:T(8,128)(2,1)}, u32[]{:S(2)}, u32[]{:S(2)}) async-start(bf16[128,1,2,8,2048]{4,3,2,1,0:T(8,128)(2,1)} %copy.62), calls=%async_computation.5 | async-start | bytes 16777216 | tf_op jit(solution)/shard_map/all_to_all | solution.py:216
  610.4 8.7 %copy-start.9 = (bf16[2,64,2048]{2,1,0:T(8,128)(2,1)S(1)}, bf16[2,64,2048]{2,1,0:T(8,128)(2,1)}, u32[]{:S(2)}) copy-start(bf16[2,64,2048]{2,1,0:T(8,128)(2,1)} %copy-done.8) | copy-start | bytes 1572868
  610.4 8.7 %copy-start.25 = (bf16[2048,64]{0,1:T(8,128)(2,1)S(1)}, bf16[2048,64]{0,1:T(8,128)(2,1)}, u32[]{:S(2)}) copy-start(bf16[2048,64]{0,1:T(8,128)(2,1)} %param.30) | copy-start | bytes 786436
  (20 other events, 87.3 us)
Sparse Core Ops, SparseCore 0:
  9.6 32.1 all-gather.10
  43.5 30.7 all-gather.8
  76.0 30.7 all-gather.6
  108.3 30.7 all-gather.4
where the time goes:
time: 772 us; the launch traced here: 760 us
  local copies, waits for them, and re-layouts  260 us (34%)
  waiting for transfers between devices  162 us (21%)
  blocking collectives  119 us (15%)
  other arithmetic  86.2 us (11%)
  matrix products  84.1 us (11%)
  starting transfers between devices  32.2 us (4%)
  between operations  15.8 us (2%)
    scatter x1, local copies, waits for them, and re-layouts, on_device(): buffer = jnp.zeros((experts_all, slots_here, most_slots, model_width), jn...  144 us
    all_to_all x1, blocking collectives, on_device(): lax.all_to_all(outgoing, ('req', 'exp'), split_axis=0, concat_axis=0, til...  107 us
    all_to_all x1, waiting for transfers between devices, on_device(): lax.all_to_all(jnp.einsum('nsrkf,sfd->nsrkd', active, down_local, preferr...  85.9 us
    all_gather x1, waiting for transfers between devices, on_device(): lax.all_gather(q_new, 'req', axis=0, tiled=True)  29.5 us
    dot_general x1, matrix products, on_device(): jnp.einsum('nsrkf,sfd->nsrkd', active, down_local, preferred_element_type...  27.3 us
    all_gather x1, waiting for transfers between devices, on_device(): lax.all_gather(k_new, 'req', axis=0, tiled=True)  26.1 us
    gather x2, local copies, waits for them, and re-layouts, on_device(): picked = summed[route_sel, slot_ids, ranks]  23.6 us
    dot_general x4, matrix products, attend_block(): jnp.einsum('qd,kd->qk', q_block, key_rows, preferred_element_type=jnp.flo...  23.1 us
  transfers between devices with their start and end apart: 9, of which 5 were waited for; matrix products, arithmetic and copies ran while one was open for 20% of the time, Pallas kernels for 0%

commit v1 on v0

v1 whole, which is shorter than its diff:
```python
import functools
import math

import jax
import jax.numpy as jnp
from jax import lax
from jax.experimental import pallas as pl
from jax.experimental.pallas import tpu as pltpu
from jax.sharding import PartitionSpec as P

SPLIT = 2
MOST = 8
BLOCK = 512
SINK_PAD = 128
GRAIN = 16


def rotary_tables(length, count, width):
    half_width = width // 2
    frequency = 10000.0 ** (-2.0 * jnp.arange(half_width, dtype=jnp.float32) / width)
    positions = length + jnp.arange(count, dtype=jnp.int32)
    angles = positions.astype(jnp.float32)[:, None] * frequency[None, :]
    cosine = jnp.cos(angles)
    sine = jnp.sin(angles)
    return (
        jnp.concatenate([cosine, cosine], axis=1),
        jnp.concatenate([-sine, sine], axis=1),
    )


def attention_kernel(
    info, arrived, cache, sink, cosine, sine, context, cache_out, k_rot, v_new, scores, shifted, top_acc, sum_acc, out_acc
):
    step = pl.program_id(0)
    length = info[1]
    window = cache.shape[2]
    rows = arrived.shape[2] // 3
    seq_len = arrived.shape[1] * rows
    width = arrived.shape[3]
    chunks = BLOCK // rows
    turn = lax.rem(length, window)

    def rotated(first_chunk, row_from, kind):
        raw = arrived[0, pl.ds(first_chunk, chunks), kind * rows : (kind + 1) * rows, :]
        raw = raw.reshape(BLOCK, width).astype(jnp.float32)
        cos_rows = cosine[pl.ds(row_from, BLOCK), :]
        sin_rows = sine[pl.ds(row_from, BLOCK), :]
        return raw * cos_rows + pltpu.roll(raw, width // 2, 1) * sin_rows

    @pl.when(step == 0)
    def _():
        for part in range(seq_len // BLOCK):
            k_rot[part * BLOCK : (part + 1) * BLOCK, :] = rotated(
                part * chunks, part * BLOCK, 1
            ).astype(jnp.bfloat16)
            v_new[part * BLOCK : (part + 1) * BLOCK, :] = arrived[
                0, part * chunks : (part + 1) * chunks, 2 * rows : 3 * rows, :
            ].reshape(BLOCK, width)
        shift = lax.rem(turn, GRAIN)
        base = turn - shift
        last = lax.rem(base + seq_len, window)
        for kind, fresh in ((0, k_rot), (1, v_new)):
            cache_out[0, kind] = cache[0, kind]
            shifted[0:GRAIN, :] = cache[
                0, kind, pl.ds(pl.multiple_of(base, GRAIN), GRAIN), :
            ].astype(jnp.float32)
            shifted[seq_len : seq_len + GRAIN, :] = cache[
                0, kind, pl.ds(pl.multiple_of(last, GRAIN), GRAIN), :
            ].astype(jnp.float32)
            shifted[pl.ds(shift, seq_len), :] = fresh[...].astype(jnp.float32)

            def place(index, carry):
                target = pl.multiple_of(lax.rem(base + index * GRAIN, window), GRAIN)
                cache_out[0, kind, pl.ds(target, GRAIN), :] = shifted[
                    pl.ds(pl.multiple_of(index * GRAIN, GRAIN), GRAIN), :
                ].astype(jnp.bfloat16)
                return carry

            lax.fori_loop(0, seq_len // GRAIN + 1, place, 0)

    first_row = step * BLOCK
    query = rotated(step * chunks, first_row, 0).astype(jnp.bfloat16)
    row_ids = first_row + lax.broadcasted_iota(jnp.int32, (BLOCK, 1), 0)
    cycle_blocks = window // BLOCK
    new_blocks = seq_len // BLOCK
    sink_block = cycle_blocks + new_blocks
    contract_last = (((1,), (1,)), ((), ()))

    def score(keys):
        return lax.dot_general(query, keys, contract_last, preferred_element_type=jnp.float32)

    def note(block, values):
        best = top_acc[...]
        for lane in range(values.shape[1] // 128):
            best = jnp.maximum(best, values[:, lane * 128 : (lane + 1) * 128])
        top_acc[...] = best
        if values.shape[1] == BLOCK:
            scores[block] = values
        else:
            scores[block, :, 0 : values.shape[1]] = values

    lowest = jnp.float32(-jnp.inf)
    top_acc[...] = jnp.full_like(top_acc, -jnp.inf)

    def order_from(block):
        return lax.rem(block * BLOCK - turn + window, window)

    def cycle_seen(block):
        end = order_from(block) + BLOCK - 1
        return (end > first_row) & (end >= window - length)

    def score_cycle(block, carry):
        start = order_from(block)
        whole = (
            (start + BLOCK <= window)
            & (start > first_row + BLOCK - 1)
            & (start >= window - length)
        )
        keys_at = pl.ds(pl.multiple_of(block * BLOCK, BLOCK), BLOCK)

        @pl.when(whole)
        def _():
            note(block, score(cache[0, 0, keys_at, :]))

        @pl.when(cycle_seen(block) & jnp.logical_not(whole))
        def _():
            order = lax.rem(start + lax.broadcasted_iota(jnp.int32, (1, BLOCK), 1), window)
            order = jnp.where(order >= window - length, order, -1)
            note(block, jnp.where(order > row_ids, score(cache[0, 0, keys_at, :]), lowest))

        return carry

    lax.fori_loop(0, cycle_blocks, score_cycle, 0)

    def score_new(block, carry):
        keys_at = pl.ds(pl.multiple_of(block * BLOCK, BLOCK), BLOCK)
        note(cycle_blocks + block, score(k_rot[keys_at, :]))
        return carry

    lax.fori_loop(0, step, score_new, 0)
    own_at = pl.ds(pl.multiple_of(first_row, BLOCK), BLOCK)
    columns = first_row + lax.broadcasted_iota(jnp.int32, (1, BLOCK), 1)
    note(cycle_blocks + step, jnp.where(columns <= row_ids, score(k_rot[own_at, :]), lowest))
    sink_columns = lax.broadcasted_iota(jnp.int32, (1, SINK_PAD), 1)
    sink_columns = jnp.where(sink_columns < info[2], sink_columns, window + 2 * seq_len + length)
    note(
        sink_block,
        jnp.where(sink_columns <= length + row_ids - window, score(sink[0, 0]), lowest),
    )

    top = jnp.max(top_acc[...], axis=1, keepdims=True)
    factor = jnp.float32(width ** (-0.5) * math.log2(math.e))

    def weights_of(values):
        return jnp.exp2((values - top) * factor)

    def add_up(weights, values):
        total = sum_acc[...]
        for lane in range(weights.shape[1] // 128):
            total = total + weights[:, lane * 128 : (lane + 1) * 128]
        sum_acc[...] = total
        out_acc[...] += jnp.dot(
            weights.astype(jnp.bfloat16), values, preferred_element_type=jnp.float32
        )

    sink_weights = weights_of(scores[sink_block, :, 0:SINK_PAD])
    sum_acc[...] = sink_weights
    out_acc[...] = jnp.dot(
        sink_weights.astype(jnp.bfloat16), sink[0, 1], preferred_element_type=jnp.float32
    )

    def blend_cycle(block, carry):
        @pl.when(cycle_seen(block))
        def _():
            add_up(
                weights_of(scores[block]),
                cache[0, 1, pl.ds(pl.multiple_of(block * BLOCK, BLOCK), BLOCK), :],
            )

        return carry

    lax.fori_loop(0, cycle_blocks, blend_cycle, 0)

    def blend_new(block, carry):
        add_up(
            weights_of(scores[cycle_blocks + block]),
            v_new[pl.ds(pl.multiple_of(block * BLOCK, BLOCK), BLOCK), :],
        )
        return carry

    lax.fori_loop(0, step + 1, blend_new, 0)
    total = jnp.sum(sum_acc[...], axis=1, keepdims=True)
    context[...] = (out_acc[...] / total).astype(jnp.bfloat16)


def attend(info, arrived, cache, sink, cosine, sine, interpret=False):
    groups, senders, rows3, width = arrived.shape
    seq_len = senders * (rows3 // 3)
    window = cache.shape[2]
    block_count = window // BLOCK + seq_len // BLOCK + 1
    once = pl.Buffered(1)
    return pl.pallas_call(
        attention_kernel,
        grid_spec=pltpu.PrefetchScalarGridSpec(
            num_scalar_prefetch=1,
            grid=(seq_len // BLOCK,),
            in_specs=[
                pl.BlockSpec((1, senders, rows3, width), lambda i, info: (info[0], 0, 0, 0), pipeline_mode=once),
                pl.BlockSpec((1, 2, window, width), lambda i, info: (0, 0, 0, 0), pipeline_mode=once),
                pl.BlockSpec((1, 2, SINK_PAD, width), lambda i, info: (0, 0, 0, 0), pipeline_mode=once),
                pl.BlockSpec((seq_len, width), lambda i, info: (0, 0), pipeline_mode=once),
                pl.BlockSpec((seq_len, width), lambda i, info: (0, 0), pipeline_mode=once),
            ],
            out_specs=[
                pl.BlockSpec((BLOCK, width), lambda i, info: (i, 0)),
                pl.BlockSpec((1, 2, window, width), lambda i, info: (0, 0, 0, 0), pipeline_mode=once),
            ],
            scratch_shapes=[
                pltpu.VMEM((seq_len, width), jnp.bfloat16),
                pltpu.VMEM((seq_len, width), jnp.bfloat16),
                pltpu.VMEM((block_count, BLOCK, BLOCK), jnp.float32),
                pltpu.VMEM((seq_len + GRAIN, width), jnp.float32),
                pltpu.VMEM((BLOCK, 128), jnp.float32),
                pltpu.VMEM((BLOCK, 128), jnp.float32),
                pltpu.VMEM((BLOCK, width), jnp.float32),
            ],
        ),
        out_shape=[
            jax.ShapeDtypeStruct((seq_len, width), jnp.bfloat16),
            jax.ShapeDtypeStruct(cache.shape, jnp.bfloat16),
        ],
        compiler_params=pltpu.CompilerParams(
            dimension_semantics=("arbitrary",), vmem_limit_bytes=48 << 20
        ),
        interpret=interpret,
        name="attend",
    )(info, arrived, cache, sink, cosine, sine)


def on_device(
    hidden,
    q_new,
    k_new,
    v_new,
    routes,
    slot_request,
    lengths,
    cycle_cache,
    sink_cache,
    w_out,
    norm_gain,
    router,
    w_gate,
    w_up,
    w_down,
):
    group_width = lax.axis_size("exp")
    group_count = lax.axis_size("req")
    devices_all = group_count * group_width
    group_index = lax.axis_index("req")
    member_index = lax.axis_index("exp")
    slots_here, local_rows, model_width = hidden.shape
    head_count = q_new.shape[1]
    head_dim = q_new.shape[3]
    experts_all = router.shape[1]
    slots_all = slot_request.shape[0]
    seq_len = local_rows * group_width
    tokens = slots_here * local_rows

    held = jnp.clip(slot_request - group_index * slots_here, 0, slots_here - 1)
    source_group = slot_request // slots_here

    def laid_out(part):
        chosen = part[0][None]
        for index in range(1, slots_here):
            flag = (held == index).reshape((slots_all,) + (1,) * (part.ndim - 1))
            chosen = jnp.where(flag, part[index][None], chosen)
        return chosen

    outgoing = laid_out(jnp.concatenate([q_new, k_new, v_new], axis=2))
    outgoing = outgoing.reshape(devices_all, 3 * local_rows, head_dim)
    arrived = lax.all_to_all(outgoing, ("req", "exp"), split_axis=0, concat_axis=0, tiled=True)
    arrived = arrived.reshape(group_count, group_width, 3 * local_rows, head_dim)

    routes_wide = jnp.pad(
        routes.astype(jnp.bfloat16), ((0, 0), (0, 0), (0, 128 - routes.shape[2]))
    )
    states = laid_out(jnp.concatenate([hidden, routes_wide], axis=2))
    states = states.reshape(group_count, tokens, model_width + 128)
    states = lax.all_to_all(states, "req", split_axis=0, concat_axis=0, tiled=True)
    states = states.reshape(group_count, slots_here, local_rows, model_width + 128)
    own_sources = lax.dynamic_slice_in_dim(
        source_group, group_index * slots_here, slots_here
    )
    states = jnp.concatenate(
        [
            lax.dynamic_index_in_dim(states[:, slot], own_sources[slot], 0, keepdims=False)
            for slot in range(slots_here)
        ],
        0,
    )
    hidden_sel = states[:, :model_width]
    route_sel = states[:, model_width : model_width + routes.shape[2]].astype(jnp.int32)

    slot_here = group_index * slots_here + member_index // head_count
    length = lax.dynamic_index_in_dim(lengths, slot_here, 0, keepdims=False)
    source = lax.dynamic_index_in_dim(source_group, slot_here, 0, keepdims=False)
    cosine, sine = rotary_tables(length, seq_len, head_dim)
    sink_count = sink_cache.shape[2]
    sink_padded = jnp.pad(sink_cache, ((0, 0), (0, 0), (0, SINK_PAD - sink_count), (0, 0)))
    info = jnp.stack([source, length, jnp.int32(sink_count)]).astype(jnp.int32)
    context, cycle_out = attend(info, arrived, cycle_cache, sink_padded, cosine, sine)

    context_rows = lax.all_to_all(
        context.reshape(group_width, local_rows, head_dim),
        "exp",
        split_axis=0,
        concat_axis=0,
        tiled=True,
    ).reshape(slots_here, head_count, local_rows, head_dim)
    context_rows = jnp.transpose(context_rows, (0, 2, 1, 3)).reshape(tokens, head_count * head_dim)
    projected = jnp.dot(context_rows, w_out, preferred_element_type=jnp.float32)
    residual = hidden_sel.astype(jnp.float32) + projected
    inverse = lax.rsqrt(jnp.mean(residual * residual, axis=-1, keepdims=True) + 1e-06)
    normed = (residual * inverse * norm_gain).astype(jnp.bfloat16)

    logits = lax.dot_general(
        router, normed, (((0,), (1,)), ((), ())), preferred_element_type=jnp.float32
    )
    expert_ids = jnp.arange(experts_all, dtype=jnp.int32)
    named = jnp.any(route_sel.T[None] == expert_ids[:, None, None], axis=1)
    token_ids = jnp.arange(tokens, dtype=jnp.int32)
    token_slot = token_ids // local_rows
    before = (token_ids[:, None] < token_ids[None, :]) & (
        token_slot[:, None] == token_slot[None, :]
    )
    ranks = jnp.dot(
        named.astype(jnp.bfloat16), before.astype(jnp.bfloat16), preferred_element_type=jnp.float32
    ).astype(jnp.int32)
    seats = jnp.arange(slots_here * MOST, dtype=jnp.int32)
    seated = named[:, None, :] & (
        token_slot[None, None, :] * MOST + ranks[:, None, :] == seats[None, :, None]
    )
    masked = jnp.where(named, logits, -jnp.inf)
    raised = jnp.exp(masked - jnp.max(masked, axis=0, keepdims=True))
    gates = raised / jnp.sum(raised, axis=0, keepdims=True)

    seats_all = experts_all * slots_here * MOST
    seating = seated.reshape(seats_all, tokens).astype(jnp.bfloat16)
    buffer = jnp.dot(seating, normed, preferred_element_type=jnp.float32).astype(jnp.bfloat16)
    received = lax.all_to_all(
        buffer.reshape(devices_all, MOST, model_width),
        ("req", "exp"),
        split_axis=0,
        concat_axis=0,
        tiled=True,
    ).reshape(devices_all * MOST, model_width)
    swap = [(index, index ^ 1) for index in range(group_width)]

    def piece(rows):
        gate_part = jnp.dot(rows, w_gate, preferred_element_type=jnp.float32)
        up_part = jnp.dot(rows, w_up, preferred_element_type=jnp.float32)
        active = (jax.nn.silu(gate_part) * up_part).astype(jnp.bfloat16)
        return jnp.dot(active, w_down, preferred_element_type=jnp.float32).astype(jnp.bfloat16)

    other_rows = lax.ppermute(received, "exp", swap)
    own_piece = piece(received)
    other_piece = lax.ppermute(piece(other_rows), "exp", swap)
    summed = (own_piece.astype(jnp.float32) + other_piece.astype(jnp.float32)).astype(jnp.bfloat16)
    returned = lax.all_to_all(
        summed.reshape(devices_all, MOST, model_width),
        ("req", "exp"),
        split_axis=0,
        concat_axis=0,
        tiled=True,
    ).reshape(seats_all, model_width)

    shares = jnp.where(seated, gates[:, None, :], 0.0).reshape(seats_all, tokens)
    coarse = lax.reduce_precision(shares, 8, 7)
    fine = (shares - coarse).astype(jnp.bfloat16)
    both = jnp.concatenate([coarse.astype(jnp.bfloat16), fine], axis=1)
    moe = lax.dot_general(
        both, returned, (((0,), (0,)), ((), ())), preferred_element_type=jnp.float32
    )
    layer_out = (residual + (moe[:tokens] + moe[tokens:])).astype(jnp.bfloat16)
    return (layer_out.reshape(slots_here, local_rows, model_width), cycle_out)


def solution(mesh):
    in_specs = (
        P("req", "exp", None),
        P("req", None, "exp", None),
        P("req", None, "exp", None),
        P("req", None, "exp", None),
        P("req", "exp", None),
        P(),
        P(),
        P(("req", "exp"), None, None, None),
        P(("req", "exp"), None, None, None),
        P(),
        P(),
        P(),
        P(None, ("req", "exp")),
        P(None, ("req", "exp")),
        P(("req", "exp"), None),
    )
    out_specs = (P("req", "exp", None), P(("req", "exp"), None, None, None))
    return jax.shard_map(
        on_device, mesh=mesh, in_specs=in_specs, out_specs=out_specs, check_vma=False
    )
```

time: 772 us -> 356 us (0.46); the launches traced: 760 us -> 352 us
  local copies, waits for them, and re-layouts: 260 us -> 19 us
  other arithmetic: 86.2 us -> 17.6 us
  blocking collectives: 119 us -> 57.4 us
  matrix products: 84.1 us -> 47.5 us
  Pallas kernels: 0 us -> 32.9 us
  waiting for transfers between devices: 162 us -> 146 us
  between operations: 15.8 us -> 4.51 us
    scatter x1 -> x0, local copies, waits for them, and re-layouts: 144 us -> none  [on_device(): buffer = jnp.zeros((experts_all, slots_here, most_slots, model_width), jn...]
    all_gather x4 -> x0, waiting for transfers between devices: 55.6 us -> none  [the longest x1 29.5 us: on_device(): lax.all_gather(q_new, 'req', axis=0, tiled=True)]
    gather x16 -> x0, local copies, waits for them, and re-layouts: 51.2 us -> none  [the longest x2 23.6 us: on_device(): picked = summed[route_sel, slot_ids, ranks]]
    all_to_all x1, blocking collectives: 107 us -> 57.4 us  [on_device(): lax.all_to_all(buffer.reshape(devices_all, MOST, model_width), ('req', 'e...]
    dot_general x20 -> x9, matrix products: 84.1 us -> 47.5 us  [the longest x2 23.5 us: piece(): jnp.dot(active, w_down, preferred_element_type=jnp.float32)]
    all_to_all x5 -> x4, waiting for transfers between devices: 104 us -> 139 us  [the longest x1 61.9 us: on_device(): lax.all_to_all(outgoing, ('req', 'exp'), split_axis=0, concat_axis=0, til...]
    pallas_call x0 -> x1, Pallas kernels: none -> 32.9 us  [attend(): pl.pallas_call(attention_kernel, grid_spec=pltpu.PrefetchScalarGridSpec(n...]
    reduce_sum x10 -> x1, other arithmetic: 28.9 us -> 0.04 us  [on_device(): gates = raised / jnp.sum(raised, axis=0, keepdims=True)]
  transfers between devices with their start and end apart: 9 -> 6, of which waited for: 5 -> 5; matrix products, arithmetic and copies ran while one was open for 20% -> 9% of each run, Pallas kernels for 0% -> 0%
where the time goes in v1:
time: 356 us; the launch traced here: 352 us
  waiting for transfers between devices  146 us (41%)
  blocking collectives  57.4 us (16%)
  matrix products  47.5 us (13%)
  Pallas kernels  32.9 us (9%)
  starting transfers between devices  27 us (8%)
  local copies, waits for them, and re-layouts  19 us (5%)
  other arithmetic  17.6 us (5%)
  between operations  4.51 us (1%)
    all_to_all x1, waiting for transfers between devices, on_device(): lax.all_to_all(outgoing, ('req', 'exp'), split_axis=0, concat_axis=0, til...  61.9 us
    all_to_all x1, blocking collectives, on_device(): lax.all_to_all(buffer.reshape(devices_all, MOST, model_width), ('req', 'e...  57.4 us
    all_to_all x1, waiting for transfers between devices, on_device(): lax.all_to_all(summed.reshape(devices_all, MOST, model_width), ('req', 'e...  49 us
    pallas_call x1, Pallas kernels, attend(): pl.pallas_call(attention_kernel, grid_spec=pltpu.PrefetchScalarGridSpec(n...  32.9 us
    dot_general x2, matrix products, piece(): jnp.dot(active, w_down, preferred_element_type=jnp.float32)  23.5 us
    all_to_all x1, waiting for transfers between devices, on_device(): lax.all_to_all(states, 'req', split_axis=0, concat_axis=0, tiled=True)  20.7 us
    dot_general x2, matrix products, piece(): gate_part = jnp.dot(rows, w_gate, preferred_element_type=jnp.float32)  12.5 us
    all_to_all x1, starting transfers between devices, on_device(): lax.all_to_all(outgoing, ('req', 'exp'), split_axis=0, concat_axis=0, til...  9.76 us
  transfers between devices with their start and end apart: 6, of which 5 were waited for; matrix products, arithmetic and copies ran while one was open for 9% of the time, Pallas kernels for 0%

profile of v1, /device:TPU:10, one launch (start us, length us, event | category | flops | bytes accessed | tf_op | source)
XLA Modules:
  0.0 352.1 jit_solution(3256936501235905002)
XLA Ops:
  4.2 1.7 bitcast_select_fusion.1
  5.9 5.1 %all-to-all-start = ((bf16[4,128,2176]{2,1,0:T(8,128)(2,1)}), bf16[4,128,2176]{2,1,0:T(8,128)(2,1)}, u32[]{:S(2)}, u32[]{:S(2)}) async-start(bf16[4,128,2176]{2,1,0:T(8,128)(2,1)} %bitcast_select_fusion.1), calls=%async_computation | async-start | bytes 4456448 | tf_op jit(solution)/shard_map/all_to_all | solution.py:290
  13.6 3.4 bitcast_select_fusion
  17.0 20.7 %all-to-all-done = bf16[4,128,2176]{2,1,0:T(8,128)(2,1)} async-done(((bf16[4,128,2176]{2,1,0:T(8,128)(2,1)}), bf16[4,128,2176]{2,1,0:T(8,128)(2,1)}, u32[]{:S(2)}, u32[]{:S(2)}) %all-to-all-start) | async-done | bytes 2228256 | tf_op jit(solution)/shard_map/all_to_all | solution.py:290
  37.7 9.8 %all-to-all-start.1 = ((bf16[128,192,128]{2,1,0:T(8,128)(2,1)}), bf16[128,192,128]{2,1,0:T(8,128)(2,1)}, u32[]{:S(2)}, u32[]{:S(2)}) async-start(bf16[128,192,128]{2,1,0:T(8,128)(2,1)} %bitcast_select_fusion), calls=%async_computation.1 | async-start | bytes 12582912 | tf_op jit(solution)/shard_map/all_to_all | solution.py:282
  55.1 3.7 %fusion.18 = (f32[2048,64]{1,0:T(8,128)S(1)}, f32[2048,64]{1,0:T(8,128)S(1)}, f32[2048,64]{1,0:T(8,128)S(1)}) fusion(f32[64]{0:T(128)S(1)} %multiply_power_fusion, f32[2048]{0:T(1024)S(1)} %add_convert_fusion.1), kind=kLoop, calls=%fused_computation.44 | loop fusion | flops 262144 | bytes 1581312 | tf_op jit(solution)/shard_map/neg | solution.py:27
  58.8 2.0 pad_maximum_fusion
  60.8 3.1 fusion.34
  63.8 61.9 %all-to-all-done.1 = bf16[128,192,128]{2,1,0:T(8,128)(2,1)} async-done(((bf16[128,192,128]{2,1,0:T(8,128)(2,1)}), bf16[128,192,128]{2,1,0:T(8,128)(2,1)}, u32[]{:S(2)}, u32[]{:S(2)}) %all-to-all-start.1) | async-done | bytes 6291488 | tf_op jit(solution)/shard_map/all_to_all | solution.py:282
  129.8 32.9 %attend.1 = (bf16[2048,128]{1,0:T(8,128)(2,1)}, bf16[1,2,4096,128]{3,2,1,0:T(8,128)(2,1)}) custom-call(s32[3]{0:T(128)S(1)} %pad_add_fusion.info, bf16[4,32,192,128]{3,2,1,0:T(8,128)(2,1)} %bitcast.13.arrived, bf16[1,2,4096,128]{3,2,1,0:T(8,128)(2,1)S(1)} %copy-done.3, bf16[1,2,128,128]{3,2,1,0:T(8,128)(2,1)S(1)} %pad.9.sink, f32[2048,128]{1,0:T(8,128)S(1)} %copy-done.1, ...), custom_call_target="tpu_custom_call" | custom-call | tf_op jit(solution)/shard_map/attend/pallas_call | solution.py:202
  162.7 4.6 %all-to-all-start.2 = ((bf16[32,64,128]{2,1,0:T(8,128)(2,1)}), bf16[32,64,128]{2,1,0:T(8,128)(2,1)}, u32[]{:S(2)}, u32[]{:S(2)}) async-start(bf16[32,64,128]{2,1,0:T(8,128)(2,1)} %bitcast.15), calls=%async_computation.2 | async-start | bytes 1048576 | tf_op jit(solution)/shard_map/all_to_all | solution.py:314
  169.6 7.4 %all-to-all-done.2 = bf16[32,64,128]{2,1,0:T(8,128)(2,1)} async-done(((bf16[32,64,128]{2,1,0:T(8,128)(2,1)}), bf16[32,64,128]{2,1,0:T(8,128)(2,1)}, u32[]{:S(2)}, u32[]{:S(2)}) %all-to-all-start.2) | async-done | bytes 524320 | tf_op jit(solution)/shard_map/all_to_all | solution.py:314
  178.4 4.8 %multiply_reduce_fusion = (f32[128]{0:T(128)S(1)}, f32[128,2048]{1,0:T(8,128)S(1)}) fusion(bf16[2048,2048]{1,0:T(8,128)(2,1)} %param.24, bf16[16,8,16,128]{3,2,1,0:T(8,128)(2,1)S(1)} %bitcast.93, bf16[64,2176]{1,0:T(8,128)(2,1)S(1)} %get-tuple-element.27, bf16[64,2176]{1,0:T(8,128)(2,1)S(1)} %get-tuple-element.28), kind=kOutput, calls=%fused_computation.26 | convolution fusion | flops 1075576704 | bytes 10519040 | tf_op jit(solution)/shard_map/dot_general | solution.py:322
  184.6 57.4 %all_to_all.25 = bf16[128,8,2048]{2,1,0:T(8,128)(2,1)S(1)} all-to-all(bf16[128,8,2048]{2,1,0:T(8,128)(2,1)S(1)} %convert_bitcast_fusion), channel_id=1, replica_groups=mesh['req'=4,'exp'=32] {'req','exp'}, dimensions={0} | all-to-all | bytes 8388608 | tf_op jit(solution)/shard_map/all_to_all | solution.py:351
  242.0 1.9 copy-done.6
  243.9 7.2 %collective-permute-done = bf16[1024,2048]{1,0:T(8,128)(2,1)S(1)} collective-permute-done((bf16[1024,2048]{1,0:T(8,128)(2,1)S(1)}, bf16[1024,2048]{1,0:T(8,128)(2,1)S(1)}, u32[]{:S(2)}, u32[]{:S(2)}) %collective-permute-start) | collective-permute-done | bytes 4194336 | tf_op jit(solution)/shard_map/ppermute | solution.py:366
  251.1 2.0 copy-done.12
  253.0 4.7 %fusion.39 = f32[1024,704]{0,1:T(8,128)} fusion(bf16[1024,2048]{1,0:T(8,128)(2,1)S(1)} %collective-permute-done, bf16[2048,704]{0,1:T(8,128)(2,1)S(1)} %copy-done.13), kind=kOutput, calls=%fused_computation.88 | convolution fusion | flops 2952790016 | bytes 9961472 | tf_op jit(solution)/shard_map/dot_general | solution.py:361
  257.8 11.2 %convolution_convert_fusion = bf16[1024,2048]{1,0:T(8,128)(2,1)} fusion(bf16[704,2048]{1,0:T(8,128)(2,1)S(1)} %copy-done, f32[1024,704]{0,1:T(8,128)} %fusion.39, bf16[1024,2048]{1,0:T(8,128)(2,1)} %copy-done.12, bf16[2048,704]{0,1:T(8,128)(2,1)} %param.28), kind=kOutput, calls=%fused_computation.6 | convolution fusion | flops 5912002560 | bytes 17039360 | tf_op jit(solution)/shard_map/dot_general | solution.py:364
  269.1 7.8 %fusion.30 = f32[1024,704]{0,1:T(8,128)} fusion(bf16[2048,704]{0,1:T(8,128)(2,1)} %param.27, bf16[128,8,2048]{2,1,0:T(8,128)(2,1)} %copy-done.6), kind=kOutput, calls=%fused_computation.80 | convolution fusion | flops 2952790016 | bytes 9961472 | tf_op jit(solution)/shard_map/dot_general | solution.py:361
  276.9 12.3 %fusion = bf16[128,8,2048]{2,1,0:T(8,128)(2,1)} fusion(bf16[1024,2048]{1,0:T(8,128)(2,1)} %collective-permute-done.1, bf16[704,2048]{1,0:T(8,128)(2,1)S(1)} %copy-done, f32[1024,704]{0,1:T(8,128)} %fusion.30, bf16[2048,704]{0,1:T(8,128)(2,1)} %param.28, bf16[128,8,2048]{2,1,0:T(8,128)(2,1)} %copy-done.6), kind=kOutput, calls=%fused_computation.2 | convolution fusion | flops 5920391168 | bytes 21233664 | tf_op jit(solution)/shard_map/dot_general | solution.py:364
  289.2 7.5 %all-to-all-start.4 = ((bf16[128,8,2048]{2,1,0:T(8,128)(2,1)}), bf16[128,8,2048]{2,1,0:T(8,128)(2,1)}, u32[]{:S(2)}, u32[]{:S(2)}) async-start(bf16[128,8,2048]{2,1,0:T(8,128)(2,1)} %fusion), calls=%async_computation.4 | async-start | bytes 8388608 | tf_op jit(solution)/shard_map/all_to_all | solution.py:370
  298.6 49.0 %all-to-all-done.4 = bf16[128,8,2048]{2,1,0:T(8,128)(2,1)} async-done(((bf16[128,8,2048]{2,1,0:T(8,128)(2,1)}), bf16[128,8,2048]{2,1,0:T(8,128)(2,1)}, u32[]{:S(2)}, u32[]{:S(2)}) %all-to-all-start.4) | async-done | bytes 4194336 | tf_op jit(solution)/shard_map/all_to_all | solution.py:370
  347.6 3.5 %fusion.1 = f32[256,2048]{1,0:T(8,128)S(1)} fusion(bf16[128,8,2048]{2,1,0:T(8,128)(2,1)} %all-to-all-done.4, bf16[1024,128]{1,0:T(8,128)(2,1)S(1)} %get-tuple-element.13, bf16[1024,128]{1,0:T(8,128)(2,1)S(1)} %get-tuple-element.12), kind=kOutput, calls=%fused_computation.3 | convolution fusion | flops 1074790400 | bytes 6815744 | tf_op jit(solution)/shard_map/dot_general | solution.py:382
  (75 shorter events, 22.1 us)
Async XLA Ops:
  0.6 257.1 %copy-start = (bf16[704,2048]{1,0:T(8,128)(2,1)S(1)}, bf16[704,2048]{1,0:T(8,128)(2,1)}, u32[]{:S(2)}) copy-start(bf16[704,2048]{1,0:T(8,128)(2,1)} %param.29) | copy-start | bytes 8650756
  5.9 5.2 %copy-start.8 = (bf16[2,16,64,128]{3,2,1,0:T(8,128)(2,1)S(1)}, bf16[2,16,64,128]{3,2,1,0:T(8,128)(2,1)}, u32[]{:S(2)}) copy-start(bf16[2,16,64,128]{3,2,1,0:T(8,128)(2,1)} %param.16) | copy-start | bytes 1572868
  5.9 31.8 %all-to-all-start = ((bf16[4,128,2176]{2,1,0:T(8,128)(2,1)}), bf16[4,128,2176]{2,1,0:T(8,128)(2,1)}, u32[]{:S(2)}, u32[]{:S(2)}) async-start(bf16[4,128,2176]{2,1,0:T(8,128)(2,1)} %bitcast_select_fusion.1), calls=%async_computation | async-start | bytes 4456448 | tf_op jit(solution)/shard_map/all_to_all | solution.py:290
  17.0 30.5 %copy-start.14 = (s32[8]{0:T(128)S(1)}, s32[8]{0:T(128)}, u32[]{:S(2)}) copy-start(s32[8]{0:T(128)} %param.20) | copy-start | bytes 100
  17.0 34.2 %copy-start.15 = (s32[8]{0:T(128)S(1)}, s32[8]{0:T(128)}, u32[]{:S(2)}) copy-start(s32[8]{0:T(128)} %param.21) | copy-start | bytes 100
  17.0 34.9 %copy-start.11 = (bf16[1,2,4,128]{3,2,1,0:T(4,128)(2,1)S(1)}, bf16[1,2,4,128]{3,2,1,0:T(4,128)(2,1)}, u32[]{:S(2)}) copy-start(bf16[1,2,4,128]{3,2,1,0:T(4,128)(2,1)} %param.23) | copy-start | bytes 6148
  37.7 88.1 %all-to-all-start.1 = ((bf16[128,192,128]{2,1,0:T(8,128)(2,1)}), bf16[128,192,128]{2,1,0:T(8,128)(2,1)}, u32[]{:S(2)}, u32[]{:S(2)}) async-start(bf16[128,192,128]{2,1,0:T(8,128)(2,1)} %bitcast_select_fusion), calls=%async_computation.1 | async-start | bytes 12582912 | tf_op jit(solution)/shard_map/all_to_all | solution.py:282
  125.8 1.2 copy-start.1
  127.0 1.2 copy-start.2
  128.2 1.6 copy-start.3
  162.7 14.3 %all-to-all-start.2 = ((bf16[32,64,128]{2,1,0:T(8,128)(2,1)}), bf16[32,64,128]{2,1,0:T(8,128)(2,1)}, u32[]{:S(2)}, u32[]{:S(2)}) async-start(bf16[32,64,128]{2,1,0:T(8,128)(2,1)} %bitcast.15), calls=%async_computation.2 | async-start | bytes 1048576 | tf_op jit(solution)/shard_map/all_to_all | solution.py:314
  178.4 4.9 %copy-start.7 = (pred[1024,128]{1,0:T(32,128)(4,1)S(1)}, pred[1024,128]{1,0:T(32,128)(4,1)}, u32[]{:S(2)}) copy-start(pred[1024,128]{1,0:T(32,128)(4,1)} %fusion.17) | copy-start | bytes 393220
  178.4 4.9 %copy-start.10 = (f32[2048]{0:T(1024)S(1)}, f32[2048]{0:T(1024)}, u32[]{:S(2)}) copy-start(f32[2048]{0:T(1024)} %param.25) | copy-start | bytes 24580
  183.2 58.7 %copy-start.4 = (f32[128,2048]{1,0:T(8,128)}, f32[128,2048]{1,0:T(8,128)S(1)}, u32[]{:S(2)}) copy-start(f32[128,2048]{1,0:T(8,128)S(1)} %get-tuple-element.20) | copy-start | bytes 3145732
  184.6 68.4 %copy-start.13 = (bf16[2048,704]{0,1:T(8,128)(2,1)S(1)}, bf16[2048,704]{0,1:T(8,128)(2,1)}, u32[]{:S(2)}) copy-start(bf16[2048,704]{0,1:T(8,128)(2,1)} %param.27) | copy-start | bytes 8650756
  242.0 1.9 copy-start.6
  243.9 7.2 %collective-permute-start = (bf16[1024,2048]{1,0:T(8,128)(2,1)S(1)}, bf16[1024,2048]{1,0:T(8,128)(2,1)S(1)}, u32[]{:S(2)}, u32[]{:S(2)}) collective-permute-start(bf16[1024,2048]{1,0:T(8,128)(2,1)S(1)} %bitcast.92), channel_id=1, source_target_pairs={{0,1},{1,0},{2,3},{3,2},{4,5},{5,4},{6,7},{7,6},{8,9},{9,8},{10,11... | collective-permute-start | bytes 12582920 | tf_op jit(solution)/shard_map/ppermute | solution.py:366
  251.1 2.0 copy-start.12
  269.0 7.9 %collective-permute-start.1 = (bf16[1024,2048]{1,0:T(8,128)(2,1)}, bf16[1024,2048]{1,0:T(8,128)(2,1)}, u32[]{:S(2)}, u32[]{:S(2)}) collective-permute-start(bf16[1024,2048]{1,0:T(8,128)(2,1)} %convolution_convert_fusion), channel_id=1, source_target_pairs={{0,1},{1,0},{2,3},{3,2},{4,5},{5,4},{6,7},{7,6},{8,9},{9,8},{10,11... | collective-permute-start | bytes 12582920 | tf_op jit(solution)/shard_map/ppermute | solution.py:368
  289.2 7.5 %copy-start.9 = (bf16[2048,64]{0,1:T(8,128)(2,1)S(1)}, bf16[2048,64]{0,1:T(8,128)(2,1)}, u32[]{:S(2)}) copy-start(bf16[2048,64]{0,1:T(8,128)(2,1)} %param.26) | copy-start | bytes 786436
  289.2 58.4 %all-to-all-start.4 = ((bf16[128,8,2048]{2,1,0:T(8,128)(2,1)}), bf16[128,8,2048]{2,1,0:T(8,128)(2,1)}, u32[]{:S(2)}, u32[]{:S(2)}) async-start(bf16[128,8,2048]{2,1,0:T(8,128)(2,1)} %fusion), calls=%async_computation.4 | async-start | bytes 8388608 | tf_op jit(solution)/shard_map/all_to_all | solution.py:370
  347.6 3.5 %copy-start.5 = (f32[128,2048]{1,0:T(8,128)S(1)}, f32[128,2048]{1,0:T(8,128)}, u32[]{:S(2)}) copy-start(f32[128,2048]{1,0:T(8,128)} %copy-done.4) | copy-start | bytes 3145732
